TPU v7x, 32 devices: a whole 2x2x4 slice. The times are simulated.
32 devices in a mesh: row: 4 (over z), col: 8 (over y, x, core).
Axes of the slice: x: 2, y: 2, z: 4, core: 2. Of those that a mesh axis runs over, the one named last changes fastest.
Arguments:
- out_grads: bfloat16 [8, 48, 28672], P('col', None, 'row'), may hold values from -6 to 6
- acts: bfloat16 [8, 48, 8192], P('row', None, 'col'), may hold values from -6 to 6
- rot_out: bfloat16 [28672, 28672], P('row', 'col'), may hold values from -0.03125 to 0.03125
- rot_in: bfloat16 [8192, 8192], P('col', 'row'), may hold values from -0.0625 to 0.0625
- queries: bfloat16 [2, 28672, 8192], P(None, 'col', 'row'), may hold values from -0.00036621094 to 0.00036621094
- token_sequence: int32 [256], replicated, may hold values from 0 to 7, never falling along the last dimension, each value on 1 to 48 neighbouring positions
Outputs:
- scores: float32 [256, 2], P(('row', 'col'))
Inputs may be any that keep to these rules, and one draw needn't show every extreme that they name: `token_sequence`: values never fall along the tokens; every sequence 0 to 7 has 1 to 48 tokens, some sequence exactly 48; the k-th token of a sequence (from 0) sits in its slot k of out_grads and acts.
All inputs are finite; a program needn't handle non-finite values.
Results may differ from a plain program's by a relative error of at most 0.0041.
Values may be sent and summed in bfloat16 or wider, within the bound.
No kernel may reach another device: no remote copies, remote signals or barrier semaphores. Data moves between devices by JAX's collectives and lax.ppermute only.
A program may use at most 128 MiB of HBM per device.

v0:
```python
import jax
import jax.numpy as jnp
from jax import lax
from jax.sharding import PartitionSpec as P


def token_places(token_sequence, seq_count, slot_count):
    token_count = token_sequence.shape[0]
    labels = jnp.arange(seq_count, dtype=jnp.int32)
    before = (token_sequence[:, None] < labels[None, :]).astype(jnp.int32)
    starts = jnp.sum(before, axis=0)
    member = (token_sequence[:, None] == labels[None, :]).astype(jnp.int32)
    own_start = jnp.sum(member * starts[None, :], axis=1)
    position = jnp.arange(token_count, dtype=jnp.int32) - own_start
    return token_sequence * slot_count + position


def local(out_grads, acts, rot_out, rot_in, queries, token_sequence):
    slot_count = out_grads.shape[1]
    seq_count = out_grads.shape[0] * lax.axis_size("col")
    flat_index = token_places(token_sequence, seq_count, slot_count)
    act_slots = lax.all_gather(acts, "row", axis=0, tiled=True)
    act_rows = jnp.take(
        act_slots.reshape(seq_count * slot_count, act_slots.shape[2]), flat_index, axis=0
    )
    grad_slots = lax.all_gather(out_grads, "col", axis=0, tiled=True)
    grad_rows = jnp.take(
        grad_slots.reshape(seq_count * slot_count, grad_slots.shape[2]), flat_index, axis=0
    )
    picked = grad_rows
    rot_grads = lax.psum(
        jnp.dot(picked, rot_out, preferred_element_type=jnp.float32), "row"
    ).astype(jnp.bfloat16)
    picked = act_rows
    rot_acts = lax.psum(jnp.dot(picked, rot_in, preferred_element_type=jnp.float32), "col").astype(
        jnp.bfloat16
    )
    projected = jnp.einsum("tj,qij->tqi", rot_acts, queries, preferred_element_type=jnp.float32)
    score_terms = jnp.sum(projected * rot_grads[:, None, :], axis=2)
    return lax.psum_scatter(score_terms, ("row", "col"), scatter_dimension=0, tiled=True)


def solution(mesh):
    placed = (
        P("col", None, "row"),
        P("row", None, "col"),
        P("row", "col"),
        P("col", "row"),
        P(None, "col", "row"),
        P(),
    )
    return jax.shard_map(
        local, mesh=mesh, in_specs=placed, out_specs=P(("row", "col"), None), check_vma=False
    )
```

profile of v0, /device:TPU:0, one launch (start us, length us, event | category | flops | bytes accessed | tf_op | source)
XLA Modules:
  0.0 327.6 jit_solution(2703172752374178728)
XLA Ops:
  6.5 0.0 all-gather.2.cloned.1.call-start
  6.5 0.7 all-gather.2.cloned.1.call-update
  7.3 0.8 convert_reduce_fusion
  8.1 0.8 select_reduce_fusion
  8.8 0.7 compare_and_fusion
  9.5 21.5 %all_gather.6 = bf16[8,48,1024]{2,1,0:T(8,128)(2,1)S(1)} all-gather(bf16[2,48,1024]{2,1,0:T(8,128)(2,1)} %param.7), channel_id=1, replica_groups=mesh['row'=4,'col'=8] {'row'}, dimensions={0}, use_global_device_ids=true | all-gather | bytes 983040 | tf_op jit(solution)/shard_map/all_gather | solution.py:22
  31.0 1.2 gather_fusion
  32.2 3.5 %fusion.6 = f32[256,2048]{1,0:T(8,128)S(1)} fusion(bf16[1024,2048]{1,0:T(8,128)(2,1)} %param.9, bf16[256,1024]{1,0:T(8,128)(2,1)S(1)} %gather_fusion, pred[256]{0:T(512)(128)(4,1)S(1)} %get-tuple-element.5), kind=kOutput, calls=%fused_computation.10 | convolution fusion | flops 1074003968 | bytes 6816000 | tf_op jit(solution)/shard_map/dot_general | solution.py:35
  35.7 65.4 %all-reduce.4 = bf16[256,2048]{1,0:T(8,128)(2,1)S(1)} all-reduce(f32[256,2048]{1,0:T(8,128)S(1)} %fusion.6), channel_id=1, replica_groups=mesh['row'=4,'col'=8] {'col'}, use_global_device_ids=true, to_apply=%region_2.3 | all-reduce | flops 524288 | bytes 3145728 | tf_op jit(solution)/shard_map/psum | solution.py:35
  101.1 0.0 all-gather.2.cloned.1.call-done
  101.1 11.3 %gather_fusion.1 = bf16[256,7168]{1,0:T(8,128)(2,1)} fusion(bf16[384,7168]{1,0:T(8,128)(2,1)} %bitcast.10, s32[1024]{0:T(1024)S(1)} %pad_clamp_fusion), kind=kCustom, calls=%fused_computation.1 | custom fusion | bytes 7341056 | tf_op jit(solution)/shard_map/jit(_take)/gather | solution.py:27
  112.5 24.3 %fusion = f32[256,3584]{1,0:T(8,128)} fusion(bf16[7168,3584]{1,0:T(8,128)(2,1)} %param.8, bf16[256,7168]{1,0:T(8,128)(2,1)} %gather_fusion.1, pred[256]{0:T(512)(128)(4,1)S(1)} %get-tuple-element.5), kind=kOutput, calls=%fused_computation.3 | convolution fusion | flops 13155172352 | bytes 58720512 | tf_op jit(solution)/shard_map/dot_general | solution.py:32
  136.8 127.4 %all-reduce.3 = bf16[256,3584]{1,0:T(8,128)(2,1)S(1)} all-reduce(f32[256,3584]{1,0:T(8,128)} %fusion), channel_id=1, replica_groups=mesh['row'=4,'col'=8] {'row'}, use_global_device_ids=true, to_apply=%region_3.4 | all-reduce | flops 917504 | bytes 5505024 | tf_op jit(solution)/shard_map/psum | solution.py:31
  264.2 2.2 convert_element_type.25
  266.4 14.7 %multiply_reduce_fusion = f32[256,2]{0,1:T(2,128)S(1)} fusion(bf16[2,3584,2048]{2,1,0:T(8,128)(2,1)} %param.10, f32[256,3584]{1,0:T(8,128)} %convert_element_type.25, bf16[256,2048]{1,0:T(8,128)(2,1)S(1)} %all-reduce.4), kind=kOutput, calls=%fused_computation.2 | convolution fusion | flops 7519862272 | bytes 34080768 | tf_op jit(solution)/shard_map/tj,qij->tqi/dot_general | solution.py:38
  281.1 39.0 %all-reduce = f32[256,2]{0,1:T(2,128)S(1)} all-reduce(f32[256,2]{0,1:T(2,128)S(1)} %multiply_reduce_fusion), channel_id=2, replica_groups=mesh['row'=4,'col'=8] {'row','col'}, use_global_device_ids=true, to_apply=%region_5.6.clone | all-reduce | flops 512 | bytes 4096
  320.1 0.6 constant_dynamic-slice_fusion
  (1 shorter events, 0.0 us)
Async XLA Ops:
  6.5 94.6 %all-gather.2.cloned.1.call-start = ((), (), s32[]{:S(2)}) async-start(), calls=%async_computation | async-start | bytes 6193152 | tf_op jit(solution)/shard_map/all_gather | solution.py:26
Sparse Core Ops, SparseCore 0:
  9.2 56.0 all-gather.1
where the time goes:
time: 328 us
  blocking collectives  253 us (77%)
  matrix products  42.5 us (13%)
  between operations  13.5 us (4%)
  local copies, waits for them, and re-layouts  13.1 us (4%)
  other arithmetic  4.48 us (1%)
    psum x1, blocking collectives, local(): lax.psum(jnp.dot(picked, rot_out, preferred_element_type=jnp.float32), 'r...  127 us
    psum x1, blocking collectives, local(): lax.psum(jnp.dot(picked, rot_in, preferred_element_type=jnp.float32), 'col')  65.4 us
    unnamed x1, blocking collectives  39 us
    dot_general x1, matrix products, local(): jnp.dot(picked, rot_out, preferred_element_type=jnp.float32)  24.3 us
    all_gather x1, blocking collectives, local(): act_slots = lax.all_gather(acts, 'row', axis=0, tiled=True)  21.5 us
    dot_general x1, matrix products, local(): jnp.einsum('tj,qij->tqi', rot_acts, queries, preferred_element_type=jnp.f...  14.7 us
    gather x1, local copies, waits for them, and re-layouts, local(): jnp.take(grad_slots.reshape(seq_count * slot_count, grad_slots.shape[2]),...  11.3 us
  transfers between devices with their start and end apart: 1, of which 0 were waited for; matrix products, arithmetic and copies ran while one was open for 2% of the time, Pallas kernels for 0%

commit v1 on v0

--- a/solution.py
+++ b/solution.py
@@ -32,9 +32,9 @@
         jnp.dot(picked, rot_out, preferred_element_type=jnp.float32), "row"
     ).astype(jnp.bfloat16)
     picked = act_rows
-    rot_acts = lax.psum(jnp.dot(picked, rot_in, preferred_element_type=jnp.float32), "col").astype(
-        jnp.bfloat16
-    )
+    rot_acts = jnp.sum(
+        lax.all_gather(jnp.dot(picked, rot_in, preferred_element_type=jnp.float32), "col"), axis=0
+    ).astype(jnp.bfloat16)
     projected = jnp.einsum("tj,qij->tqi", rot_acts, queries, preferred_element_type=jnp.float32)
     score_terms = jnp.sum(projected * rot_grads[:, None, :], axis=2)
     return lax.psum_scatter(score_terms, ("row", "col"), scatter_dimension=0, tiled=True)

time: 328 us -> 292 us (0.89)
  blocking collectives: 253 us -> 190 us
  waiting for transfers between devices: 0.73 us -> 17.7 us
  other arithmetic: 4.48 us -> 12.2 us
    psum x1 -> x0, blocking collectives: 65.4 us -> none  [local(): lax.psum(jnp.dot(picked, rot_in, preferred_element_type=jnp.float32), 'col')]
    all_gather x1, waiting for transfers between devices: 0.02 us -> 17 us  [local(): grad_slots = lax.all_gather(out_grads, 'col', axis=0, tiled=True)]
    reduce_sum x0 -> x1, other arithmetic: none -> 7.77 us  [local(): jnp.sum(lax.all_gather(jnp.dot(picked, rot_in, preferred_element_type=jnp...]
  transfers between devices with their start and end apart: 1 -> 2, of which waited for: 0 -> 1; matrix products, arithmetic and copies ran while one was open for 2% -> 16% of each run, Pallas kernels for 0% -> 0%
where the time goes in v1:
time: 292 us; the launch traced here: 291 us
  blocking collectives  190 us (65%)
  matrix products  44.5 us (15%)
  waiting for transfers between devices  17.7 us (6%)
  between operations  13.4 us (5%)
  local copies, waits for them, and re-layouts  13.1 us (4%)
  other arithmetic  12.2 us (4%)
    psum x1, blocking collectives, local(): lax.psum(jnp.dot(picked, rot_out, preferred_element_type=jnp.float32), 'r...  130 us
    unnamed x1, blocking collectives  38.2 us
    dot_general x1, matrix products, local(): jnp.dot(picked, rot_out, preferred_element_type=jnp.float32)  25 us
    all_gather x1, blocking collectives, local(): act_slots = lax.all_gather(acts, 'row', axis=0, tiled=True)  21.5 us
    all_gather x1, waiting for transfers between devices, local(): grad_slots = lax.all_gather(out_grads, 'col', axis=0, tiled=True)  17 us
    dot_general x1, matrix products, local(): jnp.einsum('tj,qij->tqi', rot_acts, queries, preferred_element_type=jnp.f...  14.7 us
    gather x1, local copies, waits for them, and re-layouts, local(): jnp.take(grad_slots.reshape(seq_count * slot_count, grad_slots.shape[2]),...  11.3 us
    reduce_sum x1, other arithmetic, local(): jnp.sum(lax.all_gather(jnp.dot(picked, rot_in, preferred_element_type=jnp...  7.77 us
  transfers between devices with their start and end apart: 2, of which 1 were waited for; matrix products, arithmetic and copies ran while one was open for 16% of the time, Pallas kernels for 0%

profile of v1, /device:TPU:0, one launch (start us, length us, event | category | flops | bytes accessed | tf_op | source)
XLA Modules:
  0.0 291.2 jit_solution(1110403547237070251)
XLA Ops:
  6.5 0.0 all-gather.4.cloned.1.call-start
  6.5 0.7 all-gather.4.cloned.1.call-update
  7.3 0.0 all-gather.6.cloned.1.call-start
  7.3 0.8 convert_reduce_fusion
  8.1 0.8 select_reduce_fusion
  8.9 0.7 compare_and_fusion
  9.6 21.5 %all_gather.12 = bf16[8,48,1024]{2,1,0:T(8,128)(2,1)S(1)} all-gather(bf16[2,48,1024]{2,1,0:T(8,128)(2,1)} %param.7), channel_id=1, replica_groups=mesh['row'=4,'col'=8] {'row'}, dimensions={0}, use_global_device_ids=true | all-gather | bytes 983040 | tf_op jit(solution)/shard_map/all_gather | solution.py:22
  31.1 1.2 gather_fusion
  32.2 4.8 %fusion.6 = f32[256,2048]{1,0:T(8,128)} fusion(bf16[1024,2048]{1,0:T(8,128)(2,1)} %param.9, bf16[256,1024]{1,0:T(8,128)(2,1)S(1)} %gather_fusion, pred[256]{0:T(512)(128)(4,1)S(1)} %get-tuple-element.5), kind=kOutput, calls=%fused_computation.10 | convolution fusion | flops 1074003968 | bytes 6816000 | tf_op jit(solution)/shard_map/dot_general | solution.py:36
  37.0 0.0 all-gather.6.cloned.1.call-update
  37.1 17.0 %all-gather.4.cloned.1.call-done = bf16[8,48,7168]{2,1,0:T(8,128)(2,1)} async-done(((bf16[1,48,7168]{2,1,0:T(8,128)(2,1)}), bf16[8,48,7168]{2,1,0:T(8,128)(2,1)}) %all-gather.4.cloned.1.call-update) | async-done | bytes 5505040 | tf_op jit(solution)/shard_map/all_gather | solution.py:26
  54.1 11.3 %gather_fusion.1 = bf16[256,7168]{1,0:T(8,128)(2,1)} fusion(bf16[384,7168]{1,0:T(8,128)(2,1)} %bitcast.11, s32[1024]{0:T(1024)S(1)} %pad_clamp_fusion), kind=kCustom, calls=%fused_computation.1 | custom fusion | bytes 7341056 | tf_op jit(solution)/shard_map/jit(_take)/gather | solution.py:27
  65.4 25.0 %fusion = f32[256,3584]{1,0:T(8,128)} fusion(bf16[7168,3584]{1,0:T(8,128)(2,1)} %param.8, bf16[256,7168]{1,0:T(8,128)(2,1)} %gather_fusion.1, pred[256]{0:T(512)(128)(4,1)S(1)} %get-tuple-element.5), kind=kOutput, calls=%fused_computation.3 | convolution fusion | flops 13155172352 | bytes 58720512 | tf_op jit(solution)/shard_map/dot_general | solution.py:32
  90.4 130.4 %all-reduce.2 = bf16[256,3584]{1,0:T(8,128)(2,1)S(1)} all-reduce(f32[256,3584]{1,0:T(8,128)} %fusion), channel_id=1, replica_groups=mesh['row'=4,'col'=8] {'row'}, use_global_device_ids=true, to_apply=%region_3.4 | all-reduce | flops 917504 | bytes 5505024 | tf_op jit(solution)/shard_map/psum | solution.py:31
  220.8 2.2 convert_element_type.25
  223.0 0.0 all-gather.6.cloned.1.call-done
  223.0 7.8 %reduce_sum.38 = bf16[256,2048]{1,0:T(8,128)(2,1)S(1)} reduce(f32[8,256,2048]{2,1,0:T(8,128)} %bitcast.13, f32[]{:T(128)} %constant.33.clone.1), dimensions={0}, to_apply=%region_2.3 | reduce | flops 3670016 | bytes 17825796 | tf_op jit(solution)/shard_map/reduce_sum | solution.py:35
  230.8 14.7 %multiply_reduce_fusion = f32[256,2]{0,1:T(2,128)S(1)} fusion(bf16[2,3584,2048]{2,1,0:T(8,128)(2,1)} %param.10, f32[256,3584]{1,0:T(8,128)} %convert_element_type.25, bf16[256,2048]{1,0:T(8,128)(2,1)S(1)} %reduce_sum.38), kind=kOutput, calls=%fused_computation.2 | convolution fusion | flops 7519862272 | bytes 34080768 | tf_op jit(solution)/shard_map/tj,qij->tqi/dot_general | solution.py:38
  245.5 38.2 %all-reduce = f32[256,2]{0,1:T(2,128)S(1)} all-reduce(f32[256,2]{0,1:T(2,128)S(1)} %multiply_reduce_fusion), channel_id=3, replica_groups=mesh['row'=4,'col'=8] {'row','col'}, use_global_device_ids=true, to_apply=%region_5.6.clone | all-reduce | flops 512 | bytes 4096
  283.7 0.6 constant_dynamic-slice_fusion
  (1 shorter events, 0.0 us)
Async XLA Ops:
  6.5 47.5 %all-gather.4.cloned.1.call-start = ((), (), s32[]{:S(2)}) async-start(), calls=%async_computation | async-start | bytes 6193152 | tf_op jit(solution)/shard_map/all_gather | solution.py:26
  7.3 215.8 %all-gather.6.cloned.1.call-start = ((), (), s32[]{:S(2)}) async-start(), calls=%async_computation.1 | async-start | bytes 18874368 | tf_op jit(solution)/shard_map/all_gather | solution.py:36
Sparse Core Ops, SparseCore 0:
  9.2 44.7 all-gather.3
  55.9 89.7 all-gather.5
